TPU v7x, 32 devices: a whole 2x2x4 slice. The times are simulated.
32 devices in a mesh: chi: 4 (over y, x), dl: 4 (over z), cell: 2 (over core).
Axes of the slice: x: 2, y: 2, z: 4, core: 2. Of those that a mesh axis runs over, the one named last changes fastest.
Arguments:
- left_env: bfloat16 [2, 512, 512, 36], P('cell', None, 'chi'), may hold values from -6 to 6
- up_left: bfloat16 [2, 512, 36, 512], P('cell', 'chi', None, 'dl'), may hold values from -0.109375 to 0.109375
- up_center: bfloat16 [2, 512, 36, 512], P('cell', 'chi', None, 'dl'), may hold values from -0.109375 to 0.109375
- right_env: bfloat16 [2, 512, 36, 512], P('cell', 'dl'), may hold values from -0.046875 to 0.046875
- center: bfloat16 [2, 512, 512], P('cell', None, 'dl'), may hold values from -0.25 to 0.25
- ket_tensor: bfloat16 [2, 6, 6, 6, 6, 2], P('cell'), may hold values from -0.875 to 0.875
Outputs:
- left_env_new: float32 [2, 512, 36, 512], P('cell', 'chi', None, 'dl')
- new_left: float32 [2, 512, 36, 512], P('cell', 'chi', None, 'dl')
All inputs are finite; a program needn't handle non-finite values.
Results may differ from a plain program's by a relative error of at most 0.0066.
The roundings to bfloat16 on the way count: a program that leaves them out, or rounds other values in their place, can miss the bound.
Values may be sent and summed in bfloat16 or wider, within the bound.
A program may use at most 256 MiB of HBM per device.

v0:
```python
import math
import jax
import jax.numpy as jnp
from jax import lax
from jax.experimental.layout import Layout, with_layout_constraint
from jax.sharding import PartitionSpec as P

ITERS = 5
HIGH = lax.Precision.HIGH
F32 = jnp.float32
BF16 = jnp.bfloat16


def from_behind(block, axis, distance):
    devices = range(lax.axis_size(axis))
    route = [((i - distance) % len(devices), i) for i in devices]
    return lax.ppermute(block, axis, route)


def pick(rows, cols, row_of, col_of):
    r = lax.broadcasted_iota(jnp.int32, (rows, cols), 0)
    c = lax.broadcasted_iota(jnp.int32, (rows, cols), 1)
    return (row_of(r) == col_of(c)).astype(BF16)


def double_layer(tensor, pad):
    leg = tensor.shape[0]
    two = leg * leg
    phys = tensor.shape[4]
    big = two * pad

    def outer(first):

        def code(n):
            m, s = (n // pad, n % pad)
            a = m // leg if first else m % leg
            b = s // leg if first else s % leg
            return jnp.where(s < two, a * leg + b, -1)

        return code

    def same(n):
        return n

    total = None
    ket_rows = pick(big, two, outer(True), same)
    bra_rows = pick(big, two, outer(False), same)
    for p in range(phys):
        mat = tensor[:, :, :, :, p].reshape(two, two)
        ket_small = jnp.dot(ket_rows, mat, preferred_element_type=F32).astype(BF16)
        bra_small = jnp.dot(bra_rows, mat, preferred_element_type=F32).astype(BF16)
        ket = lax.dot_general(
            ket_small, ket_rows, (((1,), (1,)), ((), ())), preferred_element_type=F32
        )
        bra = lax.dot_general(
            bra_small, bra_rows, (((1,), (1,)), ((), ())), preferred_element_type=F32
        )
        total = ket * bra if total is None else total + ket * bra
    return total.astype(BF16)


def row_major(block):
    return with_layout_constraint(block, Layout(major_to_minor=tuple(range(block.ndim))))


def site_input(env, stacked):
    summed = jnp.einsum("abm,csa->cmsb", env, stacked, preferred_element_type=F32).astype(BF16)
    summed = row_major(summed)
    columns, two, pad, amount = summed.shape
    return summed.reshape(columns, two * pad, amount)


def site_output(flat, layer, pad):
    out = jnp.einsum("tn,ctb->cnb", layer, flat, preferred_element_type=F32).astype(BF16)
    return out.reshape(out.shape[0], out.shape[1] // pad, pad, out.shape[2])


def spread_rows(block, pad):
    turned = jnp.pad(block.transpose(2, 1, 0), ((0, 0), (0, pad - block.shape[1]), (0, 0)))
    return lax.all_gather(row_major(turned), "chi", axis=2, tiled=True)


def shards(left_env, up_left, up_center, right_env, center, ket_tensor):
    env_local = left_env[0]
    left_iso = up_left[0]
    left_mid = up_center[0]
    env_right = right_env[0]
    bond_mat = center[0]
    site_ket = ket_tensor[0]
    chi_all = env_local.shape[0]
    leg_width = env_local.shape[2]
    pad = -(-leg_width // 8) * 8
    rows = left_iso.shape[0]
    col_count = left_iso.shape[2]
    mid_all = spread_rows(left_mid, pad)
    iso_all = spread_rows(left_iso, pad)
    next_iso = from_behind(left_iso, "cell", -1)
    bra_iso = lax.all_gather(next_iso, "dl", axis=2, tiled=True)
    layer = double_layer(site_ket, pad)
    mixed = jnp.einsum("abm,ax->bmx", env_local, bond_mat, preferred_element_type=F32).astype(BF16)
    bond_term = jnp.einsum("bma,amc->bc", mixed, env_right, preferred_element_type=F32)
    bond_slots = lax.dynamic_update_slice(
        jnp.zeros((chi_all, chi_all), F32), bond_term, (lax.axis_index("chi") * rows, 0)
    )
    mid_all, bond_slots = lax.optimization_barrier((mid_all, bond_slots))
    bond_sum = lax.psum(bond_slots, ("chi", "dl"))
    right_cut = site_output(site_input(env_local, mid_all), layer, pad)
    center_term = jnp.einsum(
        "amdb,amc->bdc", right_cut[:, :, :leg_width], env_right, preferred_element_type=F32
    ).astype(BF16)
    iso_all, center_term, bond_sum = lax.optimization_barrier((iso_all, center_term, bond_sum))
    bond_full = bond_sum.astype(BF16)
    center_part = lax.psum_scatter(center_term, "dl", scatter_dimension=0, tiled=True)
    cross_part = jnp.einsum("bdc,bdy->cy", center_part, center_part, preferred_element_type=F32)

    def env_piece(cut):
        term = jnp.einsum(
            "cmdb,bdk->kmc", cut[:, :, :leg_width], bra_iso, preferred_element_type=F32
        ).astype(BF16)
        return lax.psum_scatter(term, "chi", scatter_dimension=0, tiled=True).astype(F32)

    half = leg_width // 2 * pad
    left_flat = site_input(env_local, iso_all)
    left_early = site_output(left_flat, layer[:, :half], pad)
    left_early, left_flat, cross_part, center_part = lax.optimization_barrier(
        (left_early, left_flat, cross_part, center_part)
    )
    cross = lax.psum(cross_part, ("chi", "dl"))
    center_all = lax.all_gather(center_part, "dl", axis=0, tiled=True)
    left_late = site_output(left_flat, layer[:, half:], pad)
    env_new = jnp.concatenate([env_piece(left_early), env_piece(left_late)], axis=1)
    bond_wide = bond_full.astype(F32)
    gram = jnp.dot(jnp.dot(bond_wide, cross, precision=HIGH), bond_wide.T, precision=HIGH)
    one = jnp.eye(chi_all, dtype=F32)
    norm_sum = jnp.sum(gram * one)
    factor = 0.25 * math.sqrt(chi_all) / jnp.sqrt(norm_sum)
    gram = gram * (factor * factor)
    product = None
    for sweep_index in range(ITERS):
        step = 1.5 * one - 0.5 * gram
        product = step if product is None else jnp.dot(product, step, precision=HIGH)
        if sweep_index < ITERS - 1:
            gram = jnp.dot(jnp.dot(step, gram, precision=HIGH), step, precision=HIGH)
    mine = lax.dynamic_slice_in_dim(product, lax.axis_index("dl") * col_count, col_count, 1)
    weight = lax.dot_general(bond_wide, mine, (((0,), (0,)), ((), ())), precision=HIGH)
    weight = weight * (factor * math.sqrt(chi_all * leg_width))
    new_left = jnp.einsum("bdc,cx->bdx", center_all.astype(F32), weight, precision=HIGH)
    return (env_new[None], new_left[None])


def solution(mesh):
    placed = (
        P("cell", None, "chi", None),
        P("cell", "chi", None, "dl"),
        P("cell", "chi", None, "dl"),
        P("cell", "dl", None, None),
        P("cell", None, "dl"),
        P("cell", None, None, None, None, None),
    )
    return jax.shard_map(
        shards,
        mesh=mesh,
        in_specs=placed,
        out_specs=(P("cell", "chi", None, "dl"), P("cell", "chi", None, "dl")),
        check_vma=False,
    )
```

profile of v0, /device:TPU:0, one launch (start us, length us, event | category | flops | bytes accessed | tf_op | source)
XLA Modules:
  0.0 800.2 jit_solution(4183132327198189968)
XLA Ops:
  7.2 2.2 copy.43
  14.1 7.7 fusion.52
  21.8 11.0 %convolution_multiply_fusion.1 = f32[1440,1440]{1,0:T(8,128)} fusion(f32[1440,1440]{1,0:T(8,128)} %fusion.52, bf16[36,36]{1,0:T(8,128)(2,1)S(1)} %reshape_squeeze.6, s32[1440]{0:T(1024)S(1)} %get-tuple-element.30, s32[1440]{0:T(1024)S(1)} %get-tuple-element.33, s32[1440]{0:T(1024)S(1)} %get-tuple-element.31, s32[1440]{0:T(1024)S(1)} %get-tuple-element.32, ...), kind=kOutput, calls=%fused_computation.13 | convolution fusion | flops 157127040 | bytes 16617312 | tf_op jit(solution)/shard_map/dot_general | solution.py:55
  33.0 7.3 fusion.53
  40.3 12.5 %fusion.7 = bf16[1440,1440]{1,0:T(8,128)(2,1)} fusion(f32[1440,1440]{1,0:T(8,128)} %convolution_multiply_fusion.1, f32[1440,1440]{1,0:T(8,128)} %fusion.53, bf16[36,36]{1,0:T(8,128)(2,1)S(1)} %reshape_squeeze.7, s32[1440]{0:T(1024)S(1)} %get-tuple-element.30, s32[1440]{0:T(1024)S(1)} %get-tuple-element.33, s32[1440]{0:T(1024)S(1)} %get-tuple-element.31, ...), kind=kOutput, calls=%fused_computation.15 | convolution fusion | flops 161274240 | bytes 20764512 | tf_op jit(solution)/shard_map/dot_general | solution.py:55
  52.9 6.5 fusion.49
  59.5 15.4 %all-gather.7.cloned.1.call-done = bf16[128,40,512]{2,1,0:T(8,128)(2,1)} async-done(((bf16[128,40,128]{2,1,0:T(8,128)(2,1)}), bf16[128,40,512]{2,1,0:T(8,128)(2,1)}) %all-gather.7.cloned.1.call-update) | async-done | bytes 5242896 | tf_op jit(solution)/shard_map/all_gather | solution.py:80
  74.8 32.4 %convolution_convert_fusion.2 = bf16[128,40,128,36]{2,1,3,0:T(8,128)(2,1)} fusion(bf16[128,40,512]{2,1,0:T(8,128)(2,1)} %all-gather.7.cloned.1.call-done, bf16[1,512,128,36]{2,1,3,0:T(8,128)(2,1)} %param.6), kind=kOutput, calls=%fused_computation.4 | convolution fusion | flops 24182784000 | bytes 57147392 | tf_op jit(solution)/shard_map/abm,csa->cmsb/dot_general | solution.py:67
  107.2 98.4 %all-reduce.6 = bf16[512,512]{1,0:T(8,128)(2,1)} all-reduce(f32[512,512]{1,0:T(8,128)S(1)} %fusion.49), channel_id=1, replica_groups=mesh['chi'=4,'dl'=4,'cell'=2] {'chi','dl'}, use_global_device_ids=true, to_apply=%region_0.1 | all-reduce | flops 262144 | bytes 1572864 | tf_op jit(solution)/shard_map/psum | solution.py:106
  205.6 81.7 %convolution_convert_fusion = bf16[128,128,1440]{1,2,0:T(8,128)(2,1)} fusion(bf16[128,1440,128]{2,1,0:T(8,128)(2,1)} %bitcast.157, bf16[1440,1440]{1,0:T(8,128)(2,1)} %fusion.7), kind=kOutput, calls=%fused_computation.2 | convolution fusion | flops 67971317760 | bytes 98519040 | tf_op jit(solution)/shard_map/tn,ctb->cnb/dot_general | solution.py:74
  287.3 37.6 %fusion.10 = bf16[128,36,512]{2,0,1:T(8,128)(2,1)} fusion(bf16[1,128,36,512]{3,1,2,0:T(8,128)(2,1)S(1)} %copy-done.7, bf16[128,36,36,128]{3,2,1,0:T(8,128)(2,1)} %bitcast.158), kind=kOutput, calls=%fused_computation.18 | convolution fusion | flops 21745631232 | bytes 51904512 | tf_op jit(solution)/shard_map/amdb,amc->bdc/dot_general | solution.py:108
  326.2 2.8 collective-permute-done
  330.1 32.4 %convolution_convert_fusion.1 = bf16[128,40,128,36]{2,1,3,0:T(8,128)(2,1)} fusion(bf16[128,40,512]{2,1,0:T(8,128)(2,1)} %all-gather.5.cloned.1.call-done, bf16[1,512,128,36]{2,1,3,0:T(8,128)(2,1)} %param.6), kind=kOutput, calls=%fused_computation.3 | convolution fusion | flops 24182784000 | bytes 57147392 | tf_op jit(solution)/shard_map/abm,csa->cmsb/dot_general | solution.py:67
  362.5 45.4 %convolution_convert_fusion.4 = bf16[128,128,720]{1,2,0:T(8,128)(2,1)} fusion(bf16[128,1440,128]{2,1,0:T(8,128)(2,1)} %bitcast.155, bf16[1440,1440]{1,0:T(8,128)(2,1)} %fusion.7), kind=kOutput, calls=%fused_computation.10 | convolution fusion | flops 33985658880 | bytes 72990720 | tf_op jit(solution)/shard_map/tn,ctb->cnb/dot_general | solution.py:74
  408.0 3.6 convolution_bitcast_fusion.1
  411.6 46.5 %convolution_convert_fusion.3 = bf16[128,128,720]{1,2,0:T(8,128)(2,1)} fusion(bf16[128,1440,128]{2,1,0:T(8,128)(2,1)} %bitcast.156, bf16[1440,1440]{1,0:T(8,128)(2,1)} %fusion.7), kind=kOutput, calls=%fused_computation.9 | convolution fusion | flops 33985658880 | bytes 72990720 | tf_op jit(solution)/shard_map/tn,ctb->cnb/dot_general | solution.py:74
  458.2 41.3 %all-gather.9.cloned.1.call-done = bf16[128,36,512]{2,0,1:T(8,128)(2,1)} async-done(((bf16[128,36,128]{2,0,1:T(8,128)(2,1)}), bf16[128,36,512]{2,0,1:T(8,128)(2,1)}) %all-gather.9.cloned.1.call-update) | async-done | bytes 4718608 | tf_op jit(solution)/shard_map/all_gather | solution.py:98
  499.4 15.8 %bitcast_convert_fusion.1 = bf16[128,18,512]{2,0,1:T(8,128)(2,1)S(1)} fusion(bf16[128,36,512]{2,0,1:T(8,128)(2,1)} %all-gather.9.cloned.1.call-done, bf16[128,18,36,128]{3,2,1,0:T(8,128)(2,1)} %bitcast.160), kind=kOutput, calls=%fused_computation.19 | convolution fusion | flops 10872815616 | bytes 28311552 | tf_op jit(solution)/shard_map/cmdb,bdk->kmc/dot_general | solution.py:117
  515.2 2.4 copy.82
  517.7 15.8 %bitcast_convert_fusion.2 = bf16[128,18,512]{2,0,1:T(8,128)(2,1)S(1)} fusion(bf16[128,36,512]{2,0,1:T(8,128)(2,1)} %all-gather.9.cloned.1.call-done, bf16[128,18,40,128]{3,2,1,0:T(8,128)(2,1)} %bitcast.159), kind=kOutput, calls=%fused_computation.20 | convolution fusion | flops 10872815616 | bytes 30670848 | tf_op jit(solution)/shard_map/cmdb,bdk->kmc/dot_general | solution.py:117
  533.5 2.4 copy.80
  536.8 77.7 %all-reduce.5.cloned.1.call-done = f32[512,512]{1,0:T(8,128)} async-done(((f32[512,512]{1,0:T(8,128)}), f32[512,512]{1,0:T(8,128)}) %all-reduce.5.cloned.1.call-update) | async-done | bytes 1048592 | tf_op jit(solution)/shard_map/psum | solution.py:128
  614.5 2.0 fusion.176
  616.5 1.4 select_reduce_fusion
  628.9 1.3 fusion.55
  631.8 22.7 %reduce-scatter.12.cloned.1.call-done = bf16[128,2304]{1,0:T(8,128)(2,1)} async-done(((bf16[512,2304]{1,0:T(8,128)(2,1)}), bf16[128,2304]{1,0:T(8,128)(2,1)}) %reduce-scatter.12.cloned.1.call-update) | async-done | bytes 589840
  654.5 1.4 copy.83
  655.8 39.7 %reduce-scatter.10.cloned.1.call-done = bf16[128,2304]{1,0:T(8,128)(2,1)} async-done(((bf16[512,2304]{1,0:T(8,128)(2,1)}), bf16[128,2304]{1,0:T(8,128)(2,1)}) %reduce-scatter.10.cloned.1.call-update) | async-done | bytes 589840
  695.5 2.1 copy.81
  698.9 2.0 copy.56
  700.8 85.7 %all-gather.11.cloned.1.call-done = bf16[128,36,512]{2,0,1:T(8,128)(2,1)} async-done(((bf16[32,36,512]{2,0,1:T(8,128)(2,1)}), bf16[128,36,512]{2,0,1:T(8,128)(2,1)}) %all-gather.11.cloned.1.call-update) | async-done | bytes 4718608 | tf_op jit(solution)/shard_map/all_gather | solution.py:129
  786.5 6.3 convolution_bitcast_fusion
  (58 shorter events, 21.1 us)
Async XLA Ops:
  7.2 45.8 %copy-start = (bf16[1,512,128]{2,1,0:T(8,128)(2,1)S(1)}, bf16[1,512,128]{2,1,0:T(8,128)(2,1)}, u32[]{:S(2)}) copy-start(bf16[1,512,128]{2,1,0:T(8,128)(2,1)} %param.10) | copy-start | bytes 393220
  7.2 3.6 copy-start.3
  7.2 67.6 %all-gather.7.cloned.1.call-start = ((), (), s32[]{:S(2)}) async-start(), calls=%async_computation.4 | async-start | bytes 6553600 | tf_op jit(solution)/shard_map/all_gather | solution.py:80
  9.5 3.9 copy-start.6
  10.7 314.2 %all-gather.5.cloned.1.call-start = ((), (), s32[]{:S(2)}) async-start(), calls=%async_computation.3 | async-start | bytes 6553600 | tf_op jit(solution)/shard_map/all_gather | solution.py:80
  13.3 394.7 %reduce-scatter.8.cloned.1.call-start = ((), (), s32[]{:S(2)}) async-start(), calls=%async_computation.5 | async-start | bytes 5898240 | tf_op jit(solution)/shard_map/reduce_scatter | solution.py:113
  205.6 81.7 %copy-start.7 = (bf16[1,128,36,512]{3,1,2,0:T(8,128)(2,1)S(1)}, bf16[1,128,36,512]{3,1,2,0:T(8,128)(2,1)}, u32[]{:S(2)}) copy-start(bf16[1,128,36,512]{3,1,2,0:T(8,128)(2,1)} %param.9) | copy-start | bytes 14155780
  324.9 1.3 copy-start.4
  324.9 174.5 %all-gather.9.cloned.1.call-start = ((), (), s32[]{:S(2)}) async-start(), calls=%async_computation.6 | async-start | bytes 5898240 | tf_op jit(solution)/shard_map/all_gather | solution.py:98
  326.2 2.8 collective-permute-start
  329.0 1.0 copy-start.5
  330.1 284.4 %all-reduce.5.cloned.1.call-start = ((), (), s32[]{:S(2)}) async-start(), calls=%async_computation.8 | async-start | bytes 2097152 | tf_op jit(solution)/shard_map/psum | solution.py:128
  458.1 196.4 %reduce-scatter.12.cloned.1.call-start = ((), (), s32[]{:S(2)}) async-start(), calls=%async_computation.10 | async-start | bytes 2949120
  517.6 177.9 %reduce-scatter.10.cloned.1.call-start = ((), (), s32[]{:S(2)}) async-start(), calls=%async_computation.9 | async-start | bytes 2949120
  533.5 81.0 %copy-start.2 = (bf16[512,512]{1,0:T(8,128)(2,1)S(1)}, bf16[512,512]{1,0:T(8,128)(2,1)}, u32[]{:S(2)}) copy-start(bf16[512,512]{1,0:T(8,128)(2,1)} %all-reduce.6) | copy-start | bytes 1572868
  536.0 250.5 %all-gather.11.cloned.1.call-start = ((), (), s32[]{:S(2)}) async-start(), calls=%async_computation.7 | async-start | bytes 5898240 | tf_op jit(solution)/shard_map/all_gather | solution.py:129
  698.9 94.0 %copy-start.1 = (bf16[1,512,128]{2,1,0:T(8,128)(2,1)S(1)}, bf16[1,512,128]{2,1,0:T(8,128)(2,1)}, u32[]{:S(2)}) copy-start(bf16[1,512,128]{2,1,0:T(8,128)(2,1)} %param.10) | copy-start | bytes 393220
Sparse Core Ops, SparseCore 0:
  10.8 63.9 all-gather.6
  77.2 69.7 all-gather.4
  325.1 82.6 reduce-scatter.7
  409.7 89.6 all-gather.8
  504.6 109.8 all-reduce.4
  618.0 36.4 reduce-scatter.11
  658.1 37.3 reduce-scatter.9
  697.1 89.3 all-gather.10
where the time goes:
time: 810 us; the launch traced here: 800 us
  matrix products  379 us (47%)
  waiting for transfers between devices  286 us (35%)
  blocking collectives  98.4 us (12%)
  local copies, waits for them, and re-layouts  19.4 us (2%)
  between operations  15.5 us (2%)
    dot_general x3, matrix products, site_output(): jnp.einsum('tn,ctb->cnb', layer, flat, preferred_element_type=F32)  174 us
    psum x1, blocking collectives, shards(): bond_sum = lax.psum(bond_slots, ('chi', 'dl'))  98.4 us
    all_gather x1, waiting for transfers between devices, shards(): center_all = lax.all_gather(center_part, 'dl', axis=0, tiled=True)  85.7 us
    psum x1, waiting for transfers between devices, shards(): cross = lax.psum(cross_part, ('chi', 'dl'))  77.7 us
    dot_general x2, matrix products, site_input(): jnp.einsum('abm,csa->cmsb', env, stacked, preferred_element_type=F32)  64.8 us
    unnamed x10, waiting for transfers between devices  63 us
    all_gather x1, waiting for transfers between devices, shards(): bra_iso = lax.all_gather(next_iso, 'dl', axis=2, tiled=True)  41.3 us
    dot_general x1, matrix products, shards(): jnp.einsum('amdb,amc->bdc', right_cut[:, :, :leg_width], env_right, prefe...  37.6 us
  transfers between devices with their start and end apart: 9, of which 7 were waited for; matrix products, arithmetic and copies ran while one was open for 48% of the time, Pallas kernels for 0%

commit v1 on v0

--- a/solution.py
+++ b/solution.py
@@ -126,7 +126,19 @@
         (left_early, left_flat, cross_part, center_part)
     )
     cross = lax.psum(cross_part, ("chi", "dl"))
-    center_all = lax.all_gather(center_part, "dl", axis=0, tiled=True)
+    vals = center_part
+    local_now = lax.axis_size("dl")
+    kept_arr = lax.axis_index("dl")
+    reply, carry_out, z2 = (local_now, kept_arr, vals.shape[0])
+    steps_seen = [to_i * reply if j == 0 else to_i for j, to_i in enumerate(vals.shape)]
+    center_all = lax.dynamic_update_slice_in_dim(
+        jnp.zeros(steps_seen, vals.dtype), vals, carry_out * z2, axis=0
+    )
+    for dd in [*range(1, reply)]:
+        vals = lax.ppermute(vals, "dl", [(j, (j + 1) % reply) for j in range(reply)])
+        center_all = lax.dynamic_update_slice_in_dim(
+            center_all, vals, (carry_out - dd) % reply * z2, axis=0
+        )
     left_late = site_output(left_flat, layer[:, half:], pad)
     env_new = jnp.concatenate([env_piece(left_early), env_piece(left_late)], axis=1)
     bond_wide = bond_full.astype(F32)

time: 810 us -> 738 us (0.911)
  waiting for transfers between devices: 286 us -> 197 us
  local copies, waits for them, and re-layouts: 19.4 us -> 32.1 us
    all_gather x1 -> x0, waiting for transfers between devices: 85.7 us -> none  [shards(): center_all = lax.all_gather(center_part, 'dl', axis=0, tiled=True)]
    unnamed x10 -> x9, waiting for transfers between devices: 63 us -> 4.05 us
    ppermute x0 -> x3, waiting for transfers between devices: none -> 41.3 us  [shards(): lax.ppermute(vals, 'dl', [(j, (j + 1) % reply) for j in range(reply)])]
    all_gather x1, waiting for transfers between devices: 41.3 us -> 58.2 us  [shards(): bra_iso = lax.all_gather(next_iso, 'dl', axis=2, tiled=True)]
    dynamic_update_slice x0 -> x4, local copies, waits for them, and re-layouts: none -> 9.86 us  [the longest x3 7.36 us: shards(): lax.dynamic_update_slice_in_dim(center_all, vals, (carry_out - dd) % repl...]
  transfers between devices with their start and end apart: 9 -> 11, of which waited for: 7 -> 7; matrix products, arithmetic and copies ran while one was open for 48% -> 56% of each run, Pallas kernels for 0% -> 0%
where the time goes in v1:
time: 738 us; the launch traced here: 728 us
  matrix products  382 us (52%)
  waiting for transfers between devices  197 us (27%)
  blocking collectives  98.4 us (13%)
  local copies, waits for them, and re-layouts  32.1 us (4%)
  between operations  15.3 us (2%)
    dot_general x3, matrix products, site_output(): jnp.einsum('tn,ctb->cnb', layer, flat, preferred_element_type=F32)  174 us
    psum x1, blocking collectives, shards(): bond_sum = lax.psum(bond_slots, ('chi', 'dl'))  98.4 us
    psum x1, waiting for transfers between devices, shards(): cross = lax.psum(cross_part, ('chi', 'dl'))  75.1 us
    dot_general x2, matrix products, site_input(): jnp.einsum('abm,csa->cmsb', env, stacked, preferred_element_type=F32)  64.8 us
    all_gather x1, waiting for transfers between devices, shards(): bra_iso = lax.all_gather(next_iso, 'dl', axis=2, tiled=True)  58.2 us
    ppermute x3, waiting for transfers between devices, shards(): lax.ppermute(vals, 'dl', [(j, (j + 1) % reply) for j in range(reply)])  41.3 us
    dot_general x1, matrix products, shards(): jnp.einsum('amdb,amc->bdc', right_cut[:, :, :leg_width], env_right, prefe...  37.8 us
    dot_general x2, matrix products, env_piece(): jnp.einsum('cmdb,bdk->kmc', cut[:, :, :leg_width], bra_iso, preferred_ele...  32.1 us
  transfers between devices with their start and end apart: 11, of which 7 were waited for; matrix products, arithmetic and copies ran while one was open for 56% of the time, Pallas kernels for 0%

profile of v1, /device:TPU:0, one launch (start us, length us, event | category | flops | bytes accessed | tf_op | source)
XLA Modules:
  0.0 728.3 jit_solution(12330461004539416645)
XLA Ops:
  7.2 2.2 copy.43
  14.1 7.7 %fusion.52 = f32[1440,1440]{1,0:T(8,128)} fusion(bf16[36,36]{1,0:T(8,128)(2,1)S(1)} %reshape_squeeze.6, s32[1440]{0:T(1024)S(1)} %get-tuple-element.30, s32[1440]{0:T(1024)S(1)} %get-tuple-element.33, s32[1440]{0:T(1024)S(1)} %get-tuple-element.31, s32[1440]{0:T(1024)S(1)} %get-tuple-element.32, pred[1440]{0:T(1024)(128)(4,1)S(1)} %get-tuple-element.34, ...), kind=kOutput, calls=%fused_computation.67 | convolution fusion | flops 155468160 | bytes 8322912 | tf_op jit(solution)/shard_map/dot_general | solution.py:52
  21.8 11.0 %convolution_multiply_fusion.1 = f32[1440,1440]{1,0:T(8,128)} fusion(f32[1440,1440]{1,0:T(8,128)} %fusion.52, bf16[36,36]{1,0:T(8,128)(2,1)S(1)} %reshape_squeeze.6, s32[1440]{0:T(1024)S(1)} %get-tuple-element.30, s32[1440]{0:T(1024)S(1)} %get-tuple-element.33, s32[1440]{0:T(1024)S(1)} %get-tuple-element.31, s32[1440]{0:T(1024)S(1)} %get-tuple-element.32, ...), kind=kOutput, calls=%fused_computation.13 | convolution fusion | flops 157127040 | bytes 16617312 | tf_op jit(solution)/shard_map/dot_general | solution.py:55
  33.0 7.3 %fusion.53 = f32[1440,1440]{1,0:T(8,128)} fusion(bf16[36,36]{1,0:T(8,128)(2,1)S(1)} %reshape_squeeze.7, s32[1440]{0:T(1024)S(1)} %get-tuple-element.30, s32[1440]{0:T(1024)S(1)} %get-tuple-element.33, s32[1440]{0:T(1024)S(1)} %get-tuple-element.31, s32[1440]{0:T(1024)S(1)} %get-tuple-element.32, pred[1440]{0:T(1024)(128)(4,1)S(1)} %get-tuple-element.34, ...), kind=kOutput, calls=%fused_computation.68 | convolution fusion | flops 155468160 | bytes 8322912 | tf_op jit(solution)/shard_map/dot_general | solution.py:52
  40.3 12.4 %fusion.7 = bf16[1440,1440]{1,0:T(8,128)(2,1)} fusion(f32[1440,1440]{1,0:T(8,128)} %convolution_multiply_fusion.1, f32[1440,1440]{1,0:T(8,128)} %fusion.53, bf16[36,36]{1,0:T(8,128)(2,1)S(1)} %reshape_squeeze.7, s32[1440]{0:T(1024)S(1)} %get-tuple-element.30, s32[1440]{0:T(1024)S(1)} %get-tuple-element.33, s32[1440]{0:T(1024)S(1)} %get-tuple-element.31, ...), kind=kOutput, calls=%fused_computation.15 | convolution fusion | flops 161274240 | bytes 20764512 | tf_op jit(solution)/shard_map/dot_general | solution.py:55
  52.9 6.5 fusion.49
  59.4 15.4 %all-gather.6.cloned.1.call-done = bf16[128,40,512]{2,1,0:T(8,128)(2,1)} async-done(((bf16[128,40,128]{2,1,0:T(8,128)(2,1)}), bf16[128,40,512]{2,1,0:T(8,128)(2,1)}) %all-gather.6.cloned.1.call-update) | async-done | bytes 5242896 | tf_op jit(solution)/shard_map/all_gather | solution.py:80
  74.8 32.4 %convolution_convert_fusion.2 = bf16[128,40,128,36]{2,1,3,0:T(8,128)(2,1)} fusion(bf16[128,40,512]{2,1,0:T(8,128)(2,1)} %all-gather.6.cloned.1.call-done, bf16[1,512,128,36]{2,1,3,0:T(8,128)(2,1)} %param.6), kind=kOutput, calls=%fused_computation.4 | convolution fusion | flops 24182784000 | bytes 57147392 | tf_op jit(solution)/shard_map/abm,csa->cmsb/dot_general | solution.py:67
  107.3 98.4 %all-reduce.6 = bf16[512,512]{1,0:T(8,128)(2,1)} all-reduce(f32[512,512]{1,0:T(8,128)S(1)} %fusion.49), channel_id=1, replica_groups=mesh['chi'=4,'dl'=4,'cell'=2] {'chi','dl'}, use_global_device_ids=true, to_apply=%region_0.1 | all-reduce | flops 262144 | bytes 1572864 | tf_op jit(solution)/shard_map/psum | solution.py:106
  205.7 81.7 %convolution_convert_fusion = bf16[128,128,1440]{1,2,0:T(8,128)(2,1)} fusion(bf16[128,1440,128]{2,1,0:T(8,128)(2,1)} %bitcast.157, bf16[1440,1440]{1,0:T(8,128)(2,1)} %fusion.7), kind=kOutput, calls=%fused_computation.2 | convolution fusion | flops 67971317760 | bytes 98519040 | tf_op jit(solution)/shard_map/tn,ctb->cnb/dot_general | solution.py:74
  287.4 37.8 %fusion.10 = bf16[128,36,512]{2,0,1:T(8,128)(2,1)} fusion(bf16[1,128,36,512]{3,1,2,0:T(8,128)(2,1)S(1)} %copy-done.7, bf16[128,36,36,128]{3,2,1,0:T(8,128)(2,1)} %bitcast.158), kind=kOutput, calls=%fused_computation.18 | convolution fusion | flops 21745631232 | bytes 51904512 | tf_op jit(solution)/shard_map/amdb,amc->bdc/dot_general | solution.py:108
  326.5 2.8 collective-permute-done
  330.4 32.4 %convolution_convert_fusion.1 = bf16[128,40,128,36]{2,1,3,0:T(8,128)(2,1)} fusion(bf16[128,40,512]{2,1,0:T(8,128)(2,1)} %all-gather.4.cloned.1.call-done, bf16[1,512,128,36]{2,1,3,0:T(8,128)(2,1)} %param.6), kind=kOutput, calls=%fused_computation.3 | convolution fusion | flops 24182784000 | bytes 57147392 | tf_op jit(solution)/shard_map/abm,csa->cmsb/dot_general | solution.py:67
  362.8 45.2 %convolution_convert_fusion.4 = bf16[128,128,720]{1,2,0:T(8,128)(2,1)} fusion(bf16[128,1440,128]{2,1,0:T(8,128)(2,1)} %bitcast.155, bf16[1440,1440]{1,0:T(8,128)(2,1)} %fusion.7), kind=kOutput, calls=%fused_computation.10 | convolution fusion | flops 33985658880 | bytes 72990720 | tf_op jit(solution)/shard_map/tn,ctb->cnb/dot_general | solution.py:74
  408.1 3.6 convolution_bitcast_fusion.1
  412.7 47.0 %convolution_convert_fusion.3 = bf16[128,128,720]{1,2,0:T(8,128)(2,1)} fusion(bf16[128,1440,128]{2,1,0:T(8,128)(2,1)} %bitcast.156, bf16[1440,1440]{1,0:T(8,128)(2,1)} %fusion.7), kind=kOutput, calls=%fused_computation.9 | convolution fusion | flops 33985658880 | bytes 72990720 | tf_op jit(solution)/shard_map/tn,ctb->cnb/dot_general | solution.py:74
  459.7 58.2 %all-gather.8.cloned.1.call-done = bf16[128,36,512]{2,0,1:T(8,128)(2,1)} async-done(((bf16[128,36,128]{2,0,1:T(8,128)(2,1)}), bf16[128,36,512]{2,0,1:T(8,128)(2,1)}) %all-gather.8.cloned.1.call-update) | async-done | bytes 4718608 | tf_op jit(solution)/shard_map/all_gather | solution.py:98
  517.9 15.8 %bitcast_convert_fusion.1 = bf16[128,18,512]{2,0,1:T(8,128)(2,1)S(1)} fusion(bf16[128,36,512]{2,0,1:T(8,128)(2,1)} %all-gather.8.cloned.1.call-done, bf16[128,18,36,128]{3,2,1,0:T(8,128)(2,1)} %bitcast.160), kind=kOutput, calls=%fused_computation.19 | convolution fusion | flops 10872815616 | bytes 28311552 | tf_op jit(solution)/shard_map/cmdb,bdk->kmc/dot_general | solution.py:117
  533.7 2.4 copy.82
  536.2 16.3 %bitcast_convert_fusion.2 = bf16[128,18,512]{2,0,1:T(8,128)(2,1)S(1)} fusion(bf16[128,36,512]{2,0,1:T(8,128)(2,1)} %all-gather.8.cloned.1.call-done, bf16[128,18,40,128]{3,2,1,0:T(8,128)(2,1)} %bitcast.159), kind=kOutput, calls=%fused_computation.20 | convolution fusion | flops 10872815616 | bytes 30670848 | tf_op jit(solution)/shard_map/cmdb,bdk->kmc/dot_general | solution.py:117
  552.5 2.6 copy.80
  555.1 2.7 broadcast_in_dim.21
  557.8 2.5 constant_dynamic-update-slice_fusion.3
  560.3 75.1 %all-reduce.5.cloned.1.call-done = f32[512,512]{1,0:T(8,128)} async-done(((f32[512,512]{1,0:T(8,128)}), f32[512,512]{1,0:T(8,128)}) %all-reduce.5.cloned.1.call-update) | async-done | bytes 1048592 | tf_op jit(solution)/shard_map/psum | solution.py:128
  650.6 23.2 %collective-permute-done.2 = bf16[32,36,512]{2,0,1:T(8,128)(2,1)} collective-permute-done((bf16[32,36,512]{2,0,1:T(8,128)(2,1)}, bf16[32,36,512]{2,0,1:T(8,128)(2,1)}, u32[]{:S(2)}, u32[]{:S(2)}) %collective-permute-start.2) | collective-permute-done | bytes 1179680 | tf_op jit(solution)/shard_map/ppermute | solution.py:138
  675.9 2.2 fusion.175
  678.6 2.5 constant_dynamic-update-slice_fusion.2
  681.1 2.4 constant_dynamic-update-slice_fusion.1
  683.6 18.1 %collective-permute-done.3 = bf16[32,36,512]{2,0,1:T(8,128)(2,1)} collective-permute-done((bf16[32,36,512]{2,0,1:T(8,128)(2,1)}, bf16[32,36,512]{2,0,1:T(8,128)(2,1)}, u32[]{:S(2)}, u32[]{:S(2)}) %collective-permute-start.3) | collective-permute-done | bytes 1179680 | tf_op jit(solution)/shard_map/ppermute | solution.py:138
  701.7 2.4 constant_dynamic-update-slice_fusion
  704.1 6.5 convolution_bitcast_fusion
  712.0 3.9 reduce-scatter.10.cloned.1.call-done
  (66 shorter events, 32.0 us)
Async XLA Ops:
  7.2 45.7 %copy-start = (bf16[1,512,128]{2,1,0:T(8,128)(2,1)S(1)}, bf16[1,512,128]{2,1,0:T(8,128)(2,1)}, u32[]{:S(2)}) copy-start(bf16[1,512,128]{2,1,0:T(8,128)(2,1)} %param.10) | copy-start | bytes 393220
  7.2 3.6 copy-start.3
  7.2 67.6 %all-gather.6.cloned.1.call-start = ((), (), s32[]{:S(2)}) async-start(), calls=%async_computation.4 | async-start | bytes 6553600 | tf_op jit(solution)/shard_map/all_gather | solution.py:80
  9.5 3.9 copy-start.6
  10.7 314.5 %all-gather.4.cloned.1.call-start = ((), (), s32[]{:S(2)}) async-start(), calls=%async_computation.3 | async-start | bytes 6553600 | tf_op jit(solution)/shard_map/all_gather | solution.py:80
  13.3 394.8 %reduce-scatter.8.cloned.1.call-start = ((), (), s32[]{:S(2)}) async-start(), calls=%async_computation.5 | async-start | bytes 5898240 | tf_op jit(solution)/shard_map/reduce_scatter | solution.py:113
  205.7 81.7 %copy-start.7 = (bf16[1,128,36,512]{3,1,2,0:T(8,128)(2,1)S(1)}, bf16[1,128,36,512]{3,1,2,0:T(8,128)(2,1)}, u32[]{:S(2)}) copy-start(bf16[1,128,36,512]{3,1,2,0:T(8,128)(2,1)} %param.9) | copy-start | bytes 14155780
  325.2 1.3 copy-start.4
  325.2 192.7 %all-gather.8.cloned.1.call-start = ((), (), s32[]{:S(2)}) async-start(), calls=%async_computation.6 | async-start | bytes 5898240 | tf_op jit(solution)/shard_map/all_gather | solution.py:98
  326.5 2.8 collective-permute-start
  329.3 1.0 copy-start.5
  330.4 305.1 %all-reduce.5.cloned.1.call-start = ((), (), s32[]{:S(2)}) async-start(), calls=%async_computation.7 | async-start | bytes 2097152 | tf_op jit(solution)/shard_map/psum | solution.py:128
  411.7 233.1 %collective-permute-start.1 = (bf16[32,36,512]{2,0,1:T(8,128)(2,1)}, bf16[32,36,512]{2,0,1:T(8,128)(2,1)}, u32[]{:S(2)}, u32[]{:S(2)}) collective-permute-start(bf16[32,36,512]{2,0,1:T(8,128)(2,1)} %reduce-scatter.8.cloned.1.call-done), channel_id=1, source_target_pairs={{0,2},{2,4},{4,6},{6,0},{1,3},{3,5},{5,7},{7,1},{8,10},{10,12},{12... | collective-permute-start | bytes 3538952 | tf_op jit(solution)/shard_map/ppermute | solution.py:138
  459.7 250.9 %reduce-scatter.12.cloned.1.call-start = ((), (), s32[]{:S(2)}) async-start(), calls=%async_computation.9 | async-start | bytes 2949120
  536.2 179.8 %reduce-scatter.10.cloned.1.call-start = ((), (), s32[]{:S(2)}) async-start(), calls=%async_computation.8 | async-start | bytes 2949120
  555.1 80.3 %copy-start.2 = (bf16[512,512]{1,0:T(8,128)(2,1)S(1)}, bf16[512,512]{1,0:T(8,128)(2,1)}, u32[]{:S(2)}) copy-start(bf16[512,512]{1,0:T(8,128)(2,1)} %all-reduce.6) | copy-start | bytes 1572868
  644.7 29.0 %collective-permute-start.2 = (bf16[32,36,512]{2,0,1:T(8,128)(2,1)}, bf16[32,36,512]{2,0,1:T(8,128)(2,1)}, u32[]{:S(2)}, u32[]{:S(2)}) collective-permute-start(bf16[32,36,512]{2,0,1:T(8,128)(2,1)} %collective-permute-done.1), channel_id=1, source_target_pairs={{0,2},{2,4},{4,6},{6,0},{1,3},{3,5},{5,7},{7,1},{8,10},{10,12},{12... | collective-permute-start | bytes 3538952 | tf_op jit(solution)/shard_map/ppermute | solution.py:138
  673.8 27.9 %collective-permute-start.3 = (bf16[32,36,512]{2,0,1:T(8,128)(2,1)}, bf16[32,36,512]{2,0,1:T(8,128)(2,1)}, u32[]{:S(2)}, u32[]{:S(2)}) collective-permute-start(bf16[32,36,512]{2,0,1:T(8,128)(2,1)} %collective-permute-done.2), channel_id=1, source_target_pairs={{0,2},{2,4},{4,6},{6,0},{1,3},{3,5},{5,7},{7,1},{8,10},{10,12},{12... | collective-permute-start | bytes 3538952 | tf_op jit(solution)/shard_map/ppermute | solution.py:138
  710.6 10.6 %copy-start.1 = (bf16[1,512,128]{2,1,0:T(8,128)(2,1)S(1)}, bf16[1,512,128]{2,1,0:T(8,128)(2,1)}, u32[]{:S(2)}) copy-start(bf16[1,512,128]{2,1,0:T(8,128)(2,1)} %param.10) | copy-start | bytes 393220
Sparse Core Ops, SparseCore 0:
  10.8 63.9 all-gather.5
  77.2 69.7 all-gather.3
  325.4 82.1 reduce-scatter.7
  409.6 108.2 all-gather.7
  523.1 112.3 all-reduce.4
  639.0 36.4 reduce-scatter.11
  678.5 37.3 reduce-scatter.9
